TPU v7x, 32 devices: a whole 2x2x4 slice. The times are simulated.
32 devices in a mesh: row: 4 (over x, core), col: 8 (over z, y).
Axes of the slice: x: 2, y: 2, z: 4, core: 2. Of those that a mesh axis runs over, the one named last changes fastest.
Arguments:
- matrix: float32 [8, 512, 4, 1024], P(None, 'row', None, 'col'), as said below
Outputs:
- factored: float32 [8, 512, 4, 1024], P(None, 'row', None, 'col')
Inputs may be any that keep to these rules, and one draw needn't show every extreme that they name: `matrix`: Symmetric; an exponential covariance kernel exp(-distance / reach) between sites in three dimensions, plus a diagonal noise variance of 0.5 or more at each site, so every Schur complement taken during the factorization is positive definite.
All inputs are finite; a program needn't handle non-finite values.
Results may differ from a plain program's by a relative error of at most 0.00011.
Values sent between devices are 32-bit elements; how exact they have to be, the bound alone decides.
No kernel may reach another device: no remote copies, remote signals or barrier semaphores. Data moves between devices by JAX's collectives and lax.ppermute only.
A program may use at most 128 MiB of HBM per device.

v0:
```python
import jax
import jax.numpy as jnp
from jax import lax
from jax.sharding import PartitionSpec as P

STEPS = 8


def spread(block, axis, source):
    block = jnp.where(lax.axis_index(axis) == source, block, jnp.zeros_like(block))
    return lax.psum(block, axis)


def keep_blocks(rows_in, keep, block_size):
    blocked = rows_in.reshape(keep.shape[0], block_size, rows_in.shape[1])
    return jnp.where(keep[:, None, None], blocked, 0.0).reshape(rows_in.shape)


def pick_rows(rows_in, which, fold_ratio, block_size):
    blocked = rows_in.reshape(
        rows_in.shape[0] // (fold_ratio * block_size), fold_ratio, block_size, rows_in.shape[1]
    )
    chosen = lax.dynamic_slice_in_dim(blocked, which, 1, 1)
    return chosen.reshape(-1, rows_in.shape[1])


def product(left_rows, right_rows):
    return jnp.dot(
        left_rows, right_rows.T, precision=lax.Precision.HIGHEST, preferred_element_type=jnp.float32
    )


def finish(segment, panel_step, panel_rows, factor, row_ids, my_col, cols_dev, block_size):
    block_rows = row_ids.shape[0]
    block_count = segment.shape[1] // block_size
    blocked = segment.reshape(block_rows, block_size, block_count, block_size)
    col_here = jnp.arange(block_count, dtype=jnp.int32) * cols_dev + my_col
    below_mask = (row_ids > panel_step)[:, None, None, None]
    on_diagonal = (row_ids == panel_step)[:, None, None, None]
    written = jnp.where(
        below_mask,
        panel_rows.reshape(block_rows, block_size, 1, block_size),
        jnp.where(on_diagonal, factor[None, :, None, :], blocked),
    )
    blocked = jnp.where((col_here == panel_step)[None, None, :, None], written, blocked)
    blocked = jnp.where(on_diagonal & (col_here > panel_step)[None, None, :, None], 0.0, blocked)
    return blocked.reshape(segment.shape)


def local(matrix):
    rows_dev = lax.axis_size("row")
    cols_dev = lax.axis_size("col")
    my_row = lax.axis_index("row")
    my_col = lax.axis_index("col")
    block_rows = matrix.shape[0]
    block_size = matrix.shape[1]
    block_cols = matrix.shape[2]
    fold_ratio = cols_dev // rows_dev
    current = matrix.reshape(block_rows * block_size, block_cols * block_size)
    row_ids = jnp.arange(block_rows, dtype=jnp.int32) * rows_dev + my_row
    identity = jnp.eye(block_size, dtype=jnp.float32)
    upcoming = current[:, :block_size]
    for panel_step in range(STEPS):
        root_row = panel_step % rows_dev
        root_col = panel_step % cols_dev
        diag_first = panel_step // rows_dev * block_size
        diag_piece = upcoming[diag_first : diag_first + block_size]
        diagonal = spread(diag_piece, "row", root_row)
        factor = jnp.linalg.cholesky(diagonal)
        inverse = jax.scipy.linalg.solve_triangular(factor, identity, lower=True)
        panel_rows = keep_blocks(product(upcoming, inverse), row_ids > panel_step, block_size)
        across = spread(panel_rows, "col", root_col)
        mirrored = spread(
            pick_rows(across, my_col // rows_dev, fold_ratio, block_size), "row", my_col % rows_dev
        )
        current = finish(
            current - product(across, mirrored),
            panel_step,
            panel_rows,
            factor,
            row_ids,
            my_col,
            cols_dev,
            block_size,
        )
        next_first = (panel_step + 1) // cols_dev * block_size
        upcoming = current[:, next_first : next_first + block_size]
    return current.reshape(matrix.shape)


def solution(mesh):
    placed = (P(None, "row", None, "col"),)
    return jax.shard_map(
        local, mesh=mesh, in_specs=placed, out_specs=P(None, "row", None, "col"), check_vma=False
    )
```

profile of v0, /device:TPU:0, one launch (start us, length us, event | category | flops | bytes accessed | tf_op | source)
XLA Modules:
  0.0 1398.2 jit_solution(8074853636242637044)
XLA Ops:
  6.5 3.1 copy.114
  9.6 1.9 copy.51
  13.6 32.7 %all-reduce.25.cloned.1.call-done = f32[128,128]{0,1:T(8,128)} async-done(((f32[128,128]{0,1:T(8,128)}), f32[128,128]{0,1:T(8,128)}) %all-reduce.25.cloned.1.call-update) | async-done | bytes 65552 | tf_op jit(solution)/shard_map/psum | solution.py:11
  48.0 11.7 cholesky.134
  61.2 9.8 custom-call.12
  73.1 72.1 %all-reduce.27.cloned.1.call-done = f32[1024,128]{0,1:T(8,128)} async-done(((f32[1024,128]{0,1:T(8,128)}), f32[1024,128]{0,1:T(8,128)}) %all-reduce.27.cloned.1.call-update) | async-done | bytes 524304 | tf_op jit(solution)/shard_map/psum | solution.py:11
  145.3 1.5 reshape.577
  148.7 31.1 %all-reduce.29.cloned.1.call-done = f32[512,128]{0,1:T(8,128)} async-done(((f32[512,128]{0,1:T(8,128)}), f32[512,128]{0,1:T(8,128)}) %all-reduce.29.cloned.1.call-update) | async-done | bytes 262160 | tf_op jit(solution)/shard_map/psum | solution.py:11
  181.4 2.8 fusion.20
  185.0 31.1 %all-reduce.31.cloned.1.call-done = f32[128,128]{0,1:T(8,128)} async-done(((f32[128,128]{0,1:T(8,128)}), f32[128,128]{0,1:T(8,128)}) %all-reduce.31.cloned.1.call-update) | async-done | bytes 65552 | tf_op jit(solution)/shard_map/psum | solution.py:11
  217.9 11.7 cholesky.145
  231.1 9.8 custom-call.13
  244.3 71.6 %all-reduce.33.cloned.1.call-done = f32[1024,128]{0,1:T(8,128)} async-done(((f32[1024,128]{0,1:T(8,128)}), f32[1024,128]{0,1:T(8,128)}) %all-reduce.33.cloned.1.call-update) | async-done | bytes 524304 | tf_op jit(solution)/shard_map/psum | solution.py:11
  315.8 1.5 reshape.579
  319.1 31.2 %all-reduce.35.cloned.1.call-done = f32[512,128]{0,1:T(8,128)} async-done(((f32[512,128]{0,1:T(8,128)}), f32[512,128]{0,1:T(8,128)}) %all-reduce.35.cloned.1.call-update) | async-done | bytes 262160 | tf_op jit(solution)/shard_map/psum | solution.py:11
  351.9 2.8 fusion.17
  355.5 31.1 %all-reduce.37.cloned.1.call-done = f32[128,128]{0,1:T(8,128)} async-done(((f32[128,128]{0,1:T(8,128)}), f32[128,128]{0,1:T(8,128)}) %all-reduce.37.cloned.1.call-update) | async-done | bytes 65552 | tf_op jit(solution)/shard_map/psum | solution.py:11
  388.4 11.7 cholesky.156
  401.4 9.8 custom-call.14
  414.9 71.3 %all-reduce.39.cloned.1.call-done = f32[1024,128]{0,1:T(8,128)} async-done(((f32[1024,128]{0,1:T(8,128)}), f32[1024,128]{0,1:T(8,128)}) %all-reduce.39.cloned.1.call-update) | async-done | bytes 524304 | tf_op jit(solution)/shard_map/psum | solution.py:11
  486.2 1.5 reshape.581
  489.6 31.1 %all-reduce.41.cloned.1.call-done = f32[512,128]{0,1:T(8,128)} async-done(((f32[512,128]{0,1:T(8,128)}), f32[512,128]{0,1:T(8,128)}) %all-reduce.41.cloned.1.call-update) | async-done | bytes 262160 | tf_op jit(solution)/shard_map/psum | solution.py:11
  521.7 2.8 fusion.14
  526.5 31.2 %all-reduce.43.cloned.1.call-done = f32[128,128]{0,1:T(8,128)} async-done(((f32[128,128]{0,1:T(8,128)}), f32[128,128]{0,1:T(8,128)}) %all-reduce.43.cloned.1.call-update) | async-done | bytes 65552 | tf_op jit(solution)/shard_map/psum | solution.py:11
  559.4 11.7 cholesky.167
  572.6 9.8 custom-call.15
  582.7 2.0 fusion.29
  586.6 71.8 %all-reduce.45.cloned.1.call-done = f32[1024,128]{0,1:T(8,128)} async-done(((f32[1024,128]{0,1:T(8,128)}), f32[1024,128]{0,1:T(8,128)}) %all-reduce.45.cloned.1.call-update) | async-done | bytes 524304 | tf_op jit(solution)/shard_map/psum | solution.py:11
  658.4 1.5 reshape.583
  661.7 31.2 %all-reduce.47.cloned.1.call-done = f32[512,128]{0,1:T(8,128)} async-done(((f32[512,128]{0,1:T(8,128)}), f32[512,128]{0,1:T(8,128)}) %all-reduce.47.cloned.1.call-update) | async-done | bytes 262160 | tf_op jit(solution)/shard_map/psum | solution.py:11
  693.8 2.8 fusion.11
  698.7 31.2 %all-reduce.49.cloned.1.call-done = f32[128,128]{0,1:T(8,128)} async-done(((f32[128,128]{0,1:T(8,128)}), f32[128,128]{0,1:T(8,128)}) %all-reduce.49.cloned.1.call-update) | async-done | bytes 65552 | tf_op jit(solution)/shard_map/psum | solution.py:11
  731.6 11.7 cholesky.178
  744.8 9.8 custom-call.16
  754.9 2.0 fusion.27
  758.6 72.0 %all-reduce.51.cloned.1.call-done = f32[1024,128]{0,1:T(8,128)} async-done(((f32[1024,128]{0,1:T(8,128)}), f32[1024,128]{0,1:T(8,128)}) %all-reduce.51.cloned.1.call-update) | async-done | bytes 524304 | tf_op jit(solution)/shard_map/psum | solution.py:11
  830.6 1.5 reshape.585
  834.3 30.8 %all-reduce.53.cloned.1.call-done = f32[512,128]{0,1:T(8,128)} async-done(((f32[512,128]{0,1:T(8,128)}), f32[512,128]{0,1:T(8,128)}) %all-reduce.53.cloned.1.call-update) | async-done | bytes 262160 | tf_op jit(solution)/shard_map/psum | solution.py:11
  866.7 2.8 fusion.8
  870.2 31.1 %all-reduce.55.cloned.1.call-done = f32[128,128]{0,1:T(8,128)} async-done(((f32[128,128]{0,1:T(8,128)}), f32[128,128]{0,1:T(8,128)}) %all-reduce.55.cloned.1.call-update) | async-done | bytes 65552 | tf_op jit(solution)/shard_map/psum | solution.py:11
  903.1 11.7 cholesky.189
  916.2 9.8 custom-call.17
  929.9 71.1 %all-reduce.57.cloned.1.call-done = f32[1024,128]{0,1:T(8,128)} async-done(((f32[1024,128]{0,1:T(8,128)}), f32[1024,128]{0,1:T(8,128)}) %all-reduce.57.cloned.1.call-update) | async-done | bytes 524304 | tf_op jit(solution)/shard_map/psum | solution.py:11
  1004.2 31.2 %all-reduce.59.cloned.1.call-done = f32[512,128]{0,1:T(8,128)} async-done(((f32[512,128]{0,1:T(8,128)}), f32[512,128]{0,1:T(8,128)}) %all-reduce.59.cloned.1.call-update) | async-done | bytes 262160 | tf_op jit(solution)/shard_map/psum | solution.py:11
  1036.4 2.8 fusion.5
  1041.2 31.1 %all-reduce.61.cloned.1.call-done = f32[128,128]{0,1:T(8,128)} async-done(((f32[128,128]{0,1:T(8,128)}), f32[128,128]{0,1:T(8,128)}) %all-reduce.61.cloned.1.call-update) | async-done | bytes 65552 | tf_op jit(solution)/shard_map/psum | solution.py:11
  1074.1 11.7 cholesky.200
  1087.3 9.8 custom-call.18
  1097.4 2.0 fusion.23
  1101.1 72.0 %all-reduce.63.cloned.1.call-done = f32[1024,128]{0,1:T(8,128)} async-done(((f32[1024,128]{0,1:T(8,128)}), f32[1024,128]{0,1:T(8,128)}) %all-reduce.63.cloned.1.call-update) | async-done | bytes 524304 | tf_op jit(solution)/shard_map/psum | solution.py:11
  1176.6 31.1 %all-reduce.65.cloned.1.call-done = f32[512,128]{0,1:T(8,128)} async-done(((f32[512,128]{0,1:T(8,128)}), f32[512,128]{0,1:T(8,128)}) %all-reduce.65.cloned.1.call-update) | async-done | bytes 262160 | tf_op jit(solution)/shard_map/psum | solution.py:11
  1208.6 2.8 fusion.2
  1213.4 31.1 %all-reduce.67.cloned.1.call-done = f32[128,128]{0,1:T(8,128)} async-done(((f32[128,128]{0,1:T(8,128)}), f32[128,128]{0,1:T(8,128)}) %all-reduce.67.cloned.1.call-update) | async-done | bytes 65552 | tf_op jit(solution)/shard_map/psum | solution.py:11
  1246.3 11.7 cholesky.211
  1259.5 9.8 custom-call.19
  1269.6 2.0 fusion.21
  1273.4 71.9 %all-reduce.69.cloned.1.call-done = f32[1024,128]{0,1:T(8,128)} async-done(((f32[1024,128]{0,1:T(8,128)}), f32[1024,128]{0,1:T(8,128)}) %all-reduce.69.cloned.1.call-update) | async-done | bytes 524304 | tf_op jit(solution)/shard_map/psum | solution.py:11
  1345.3 2.4 reshape.591
  1347.7 1.9 fusion.45
  1352.5 29.2 %all-reduce.71.cloned.1.call-done = f32[512,128]{0,1:T(8,128)} async-done(((f32[512,128]{0,1:T(8,128)}), f32[512,128]{0,1:T(8,128)}) %all-reduce.71.cloned.1.call-update) | async-done | bytes 262160 | tf_op jit(solution)/shard_map/psum | solution.py:11
  1381.7 2.8 subtract_bitcast_fusion
  1384.6 1.8 copy.83
  1386.3 2.3 copy.41
  1388.6 2.2 select_select_fusion
  (303 shorter events, 85.9 us)
Async XLA Ops:
  6.5 39.7 %all-reduce.25.cloned.1.call-start = ((), (), s32[]{:S(2)}) async-start(), calls=%async_computation | async-start | bytes 131072 | tf_op jit(solution)/shard_map/psum | solution.py:11
  11.5 61.5 %copy-start.8 = (f32[1024,512]{0,1:T(8,128)}, f32[1024,512]{0,1:T(8,128)S(1)}, u32[]{:S(2)}) copy-start(f32[1024,512]{0,1:T(8,128)S(1)} %copy.51) | copy-start | bytes 6291460
  12.3 133.0 %all-reduce.27.cloned.1.call-start = ((), (), s32[]{:S(2)}) async-start(), calls=%async_computation.1 | async-start | bytes 1048576 | tf_op jit(solution)/shard_map/psum | solution.py:11
  72.7 107.1 %all-reduce.29.cloned.1.call-start = ((), (), s32[]{:S(2)}) async-start(), calls=%async_computation.2 | async-start | bytes 524288 | tf_op jit(solution)/shard_map/psum | solution.py:11
  148.3 67.8 %all-reduce.31.cloned.1.call-start = ((), (), s32[]{:S(2)}) async-start(), calls=%async_computation.3 | async-start | bytes 131072 | tf_op jit(solution)/shard_map/psum | solution.py:11
  148.7 31.6 %copy-start.12 = (f32[1024,128]{0,1:T(8,128)S(1)}, f32[1024,128]{0,1:T(8,128)}, u32[]{:S(2)}) copy-start(f32[1024,128]{0,1:T(8,128)} %all-reduce.27.cloned.1.call-done) | copy-start | bytes 1572868
  179.8 1.6 copy-start.9
  179.8 1.6 copy-start.22
  184.2 59.1 %copy-start.4 = (f32[1024,512]{0,1:T(8,128)}, f32[1024,512]{0,1:T(8,128)S(1)}, u32[]{:S(2)}) copy-start(f32[1024,512]{0,1:T(8,128)S(1)} %fusion.20) | copy-start | bytes 6291460
  184.9 130.9 %all-reduce.33.cloned.1.call-start = ((), (), s32[]{:S(2)}) async-start(), calls=%async_computation.4 | async-start | bytes 1048576 | tf_op jit(solution)/shard_map/psum | solution.py:11
  243.3 107.0 %all-reduce.35.cloned.1.call-start = ((), (), s32[]{:S(2)}) async-start(), calls=%async_computation.5 | async-start | bytes 524288 | tf_op jit(solution)/shard_map/psum | solution.py:11
  318.9 67.7 %all-reduce.37.cloned.1.call-start = ((), (), s32[]{:S(2)}) async-start(), calls=%async_computation.6 | async-start | bytes 131072 | tf_op jit(solution)/shard_map/psum | solution.py:11
  319.1 31.7 %copy-start.17 = (f32[1024,128]{0,1:T(8,128)S(1)}, f32[1024,128]{0,1:T(8,128)}, u32[]{:S(2)}) copy-start(f32[1024,128]{0,1:T(8,128)} %all-reduce.33.cloned.1.call-done) | copy-start | bytes 1572868
  350.3 1.6 copy-start.5
  350.3 1.6 copy-start.23
  355.4 130.8 %all-reduce.39.cloned.1.call-start = ((), (), s32[]{:S(2)}) async-start(), calls=%async_computation.7 | async-start | bytes 1048576 | tf_op jit(solution)/shard_map/psum | solution.py:11
  413.6 107.1 %all-reduce.41.cloned.1.call-start = ((), (), s32[]{:S(2)}) async-start(), calls=%async_computation.8 | async-start | bytes 524288 | tf_op jit(solution)/shard_map/psum | solution.py:11
  414.8 74.6 %copy-start.20 = (f32[8,128,128]{1,0,2:T(8,128)S(1)}, f32[8,128,128]{1,0,2:T(8,128)}, u32[]{:S(2)}) copy-start(f32[8,128,128]{1,0,2:T(8,128)} %copy.12) | copy-start | bytes 1572868
  489.3 68.4 %all-reduce.43.cloned.1.call-start = ((), (), s32[]{:S(2)}) async-start(), calls=%async_computation.9 | async-start | bytes 131072 | tf_op jit(solution)/shard_map/psum | solution.py:11
  489.6 31.6 %copy-start.13 = (f32[1024,128]{0,1:T(8,128)S(1)}, f32[1024,128]{0,1:T(8,128)}, u32[]{:S(2)}) copy-start(f32[1024,128]{0,1:T(8,128)} %all-reduce.39.cloned.1.call-done) | copy-start | bytes 1572868
  520.7 0.9 copy-start.24
  524.4 1.3 copy-start
  526.4 132.0 %all-reduce.45.cloned.1.call-start = ((), (), s32[]{:S(2)}) async-start(), calls=%async_computation.10 | async-start | bytes 1048576 | tf_op jit(solution)/shard_map/psum | solution.py:11
  585.9 107.0 %all-reduce.47.cloned.1.call-start = ((), (), s32[]{:S(2)}) async-start(), calls=%async_computation.11 | async-start | bytes 524288 | tf_op jit(solution)/shard_map/psum | solution.py:11
  661.5 68.3 %all-reduce.49.cloned.1.call-start = ((), (), s32[]{:S(2)}) async-start(), calls=%async_computation.12 | async-start | bytes 131072 | tf_op jit(solution)/shard_map/psum | solution.py:11
  661.7 31.7 %copy-start.1 = (f32[1024,512]{0,1:T(8,128)S(1)}, f32[1024,512]{0,1:T(8,128)}, u32[]{:S(2)}) copy-start(f32[1024,512]{0,1:T(8,128)} %copy-done) | copy-start | bytes 6291460
  661.7 31.7 %copy-start.14 = (f32[1024,128]{0,1:T(8,128)S(1)}, f32[1024,128]{0,1:T(8,128)}, u32[]{:S(2)}) copy-start(f32[1024,128]{0,1:T(8,128)} %all-reduce.45.cloned.1.call-done) | copy-start | bytes 1572868
  692.9 0.9 copy-start.25
  696.6 1.3 copy-start.6
  698.6 132.0 %all-reduce.51.cloned.1.call-start = ((), (), s32[]{:S(2)}) async-start(), calls=%async_computation.13 | async-start | bytes 1048576 | tf_op jit(solution)/shard_map/psum | solution.py:11
  758.0 107.0 %all-reduce.53.cloned.1.call-start = ((), (), s32[]{:S(2)}) async-start(), calls=%async_computation.14 | async-start | bytes 524288 | tf_op jit(solution)/shard_map/psum | solution.py:11
  833.7 67.7 %all-reduce.55.cloned.1.call-start = ((), (), s32[]{:S(2)}) async-start(), calls=%async_computation.15 | async-start | bytes 131072 | tf_op jit(solution)/shard_map/psum | solution.py:11
  834.3 31.3 %copy-start.18 = (f32[1024,128]{0,1:T(8,128)S(1)}, f32[1024,128]{0,1:T(8,128)}, u32[]{:S(2)}) copy-start(f32[1024,128]{0,1:T(8,128)} %all-reduce.51.cloned.1.call-done) | copy-start | bytes 1572868
  865.1 1.6 copy-start.7
  865.1 1.6 copy-start.26
  870.1 130.8 %all-reduce.57.cloned.1.call-start = ((), (), s32[]{:S(2)}) async-start(), calls=%async_computation.16 | async-start | bytes 1048576 | tf_op jit(solution)/shard_map/psum | solution.py:11
  928.4 107.0 %all-reduce.59.cloned.1.call-start = ((), (), s32[]{:S(2)}) async-start(), calls=%async_computation.17 | async-start | bytes 524288 | tf_op jit(solution)/shard_map/psum | solution.py:11
  929.8 74.3 %copy-start.21 = (f32[8,128,128]{1,0,2:T(8,128)S(1)}, f32[8,128,128]{1,0,2:T(8,128)}, u32[]{:S(2)}) copy-start(f32[8,128,128]{1,0,2:T(8,128)} %copy.27) | copy-start | bytes 1572868
  1004.0 68.3 %all-reduce.61.cloned.1.call-start = ((), (), s32[]{:S(2)}) async-start(), calls=%async_computation.18 | async-start | bytes 131072 | tf_op jit(solution)/shard_map/psum | solution.py:11
  1004.2 31.7 %copy-start.15 = (f32[1024,128]{0,1:T(8,128)S(1)}, f32[1024,128]{0,1:T(8,128)}, u32[]{:S(2)}) copy-start(f32[1024,128]{0,1:T(8,128)} %all-reduce.57.cloned.1.call-done) | copy-start | bytes 1572868
  1035.4 0.9 copy-start.27
  1039.1 1.3 copy-start.2
  1041.1 132.0 %all-reduce.63.cloned.1.call-start = ((), (), s32[]{:S(2)}) async-start(), calls=%async_computation.19 | async-start | bytes 1048576 | tf_op jit(solution)/shard_map/psum | solution.py:11
  1100.5 107.1 %all-reduce.65.cloned.1.call-start = ((), (), s32[]{:S(2)}) async-start(), calls=%async_computation.20 | async-start | bytes 524288 | tf_op jit(solution)/shard_map/psum | solution.py:11
  1176.2 68.4 %all-reduce.67.cloned.1.call-start = ((), (), s32[]{:S(2)}) async-start(), calls=%async_computation.21 | async-start | bytes 131072 | tf_op jit(solution)/shard_map/psum | solution.py:11
  1176.5 31.6 %copy-start.3 = (f32[1024,512]{0,1:T(8,128)S(1)}, f32[1024,512]{0,1:T(8,128)}, u32[]{:S(2)}) copy-start(f32[1024,512]{0,1:T(8,128)} %copy-done.2) | copy-start | bytes 6291460
  1176.5 31.6 %copy-start.16 = (f32[1024,128]{0,1:T(8,128)S(1)}, f32[1024,128]{0,1:T(8,128)}, u32[]{:S(2)}) copy-start(f32[1024,128]{0,1:T(8,128)} %all-reduce.63.cloned.1.call-done) | copy-start | bytes 1572868
  1207.6 0.9 copy-start.28
  1211.3 1.3 copy-start.10
  1213.3 132.0 %all-reduce.69.cloned.1.call-start = ((), (), s32[]{:S(2)}) async-start(), calls=%async_computation.22 | async-start | bytes 1048576 | tf_op jit(solution)/shard_map/psum | solution.py:11
  1272.7 109.0 %all-reduce.71.cloned.1.call-start = ((), (), s32[]{:S(2)}) async-start(), calls=%async_computation.23 | async-start | bytes 524288 | tf_op jit(solution)/shard_map/psum | solution.py:11
  1273.4 108.3 %copy-start.11 = (f32[1024,512]{0,1:T(8,128)S(1)}, f32[1024,512]{0,1:T(8,128)}, u32[]{:S(2)}) copy-start(f32[1024,512]{0,1:T(8,128)} %copy-done.10) | copy-start | bytes 6291460
  1345.3 36.4 %copy-start.19 = (f32[1024,128]{0,1:T(8,128)S(1)}, f32[1024,128]{0,1:T(8,128)}, u32[]{:S(2)}) copy-start(f32[1024,128]{0,1:T(8,128)} %all-reduce.69.cloned.1.call-done) | copy-start | bytes 1572868
Sparse Core Ops, SparseCore 0:
  12.4 33.7 all-reduce.24
  72.8 72.3 all-reduce.26
  148.4 31.2 all-reduce.28
  185.0 31.0 all-reduce.30
  243.4 72.3 all-reduce.32
  319.0 31.2 all-reduce.34
  355.5 31.0 all-reduce.36
  413.8 72.3 all-reduce.38
  489.4 31.2 all-reduce.40
  526.5 31.0 all-reduce.42
  586.0 72.4 all-reduce.44
  661.6 31.2 all-reduce.46
  698.7 31.0 all-reduce.48
  758.2 72.3 all-reduce.50
  833.8 31.2 all-reduce.52
  870.3 31.0 all-reduce.54
  928.5 72.3 all-reduce.56
  1004.1 31.2 all-reduce.58
  1041.2 31.0 all-reduce.60
  1100.7 72.3 all-reduce.62
  1176.3 31.2 all-reduce.64
  1213.4 31.0 all-reduce.66
  1272.9 72.3 all-reduce.68
  1350.4 31.2 all-reduce.70
where the time goes:
time: 1410 us; the launch traced here: 1400 us
  waiting for transfers between devices  1070 us (76%)
  other arithmetic  214 us (15%)
  local copies, waits for them, and re-layouts  56.8 us (4%)
  matrix products  37.2 us (3%)
  between operations  15.4 us (1%)
    psum x24, waiting for transfers between devices, spread(): return lax.psum(block, axis)  1070 us
    another operation x24, other arithmetic, local(): factor = jnp.linalg.cholesky(diagonal)  99.6 us
    another operation x16, other arithmetic, local(): inverse = jax.scipy.linalg.solve_triangular(factor, identity, lower=True)  84 us
    dot_general x16, matrix products, product(): jnp.dot(left_rows, right_rows.T, precision=lax.Precision.HIGHEST, preferr...  34.9 us
  transfers between devices with their start and end apart: 24, of which 24 were waited for; matrix products, arithmetic and copies ran while one was open for 1% of the time, Pallas kernels for 0%

commit v1 on v0

--- a/solution.py
+++ b/solution.py
@@ -8,7 +8,8 @@
 
 def spread(block, axis, source):
     block = jnp.where(lax.axis_index(axis) == source, block, jnp.zeros_like(block))
-    return lax.psum(block, axis)
+    _launch_types = lambda x_local, named_axis: lax.all_gather(x_local, named_axis).sum(axis=0)
+    return _launch_types(block, axis)
 
 
 def keep_blocks(rows_in, keep, block_size):

time: 1410 us -> 1100 us (0.78)
  waiting for transfers between devices: 1070 us -> 690 us
  blocking collectives: 0 us -> 49.2 us
  local copies, waits for them, and re-layouts: 56.8 us -> 84.9 us
    psum x24 -> x0, waiting for transfers between devices: 1070 us -> none  [spread(): return lax.psum(block, axis)]
    all_gather x0 -> x16, waiting for transfers between devices: none -> 690 us  [spread(): lax.all_gather(x_local, named_axis).sum(axis=0)]
    all_gather x0 -> x8, blocking collectives: none -> 49.2 us  [spread(): lax.all_gather(x_local, named_axis).sum(axis=0)]
    unnamed x69 -> x28, local copies, waits for them, and re-layouts: 21.1 us -> 51 us
    reduce_sum x0 -> x24, other arithmetic: none -> 18.6 us  [spread(): lax.all_gather(x_local, named_axis).sum(axis=0)]
  transfers between devices with their start and end apart: 24 -> 16, of which waited for: 24 -> 16; matrix products, arithmetic and copies ran while one was open for 1% -> 2% of each run, Pallas kernels for 0% -> 0%
where the time goes in v1:
time: 1100 us
  waiting for transfers between devices  690 us (63%)
  other arithmetic  223 us (20%)
  local copies, waits for them, and re-layouts  84.9 us (8%)
  blocking collectives  49.2 us (4%)
  matrix products  31.8 us (3%)
  between operations  15.2 us (1%)
    all_gather x16, waiting for transfers between devices, spread(): lax.all_gather(x_local, named_axis).sum(axis=0)  690 us
    another operation x24, other arithmetic, local(): factor = jnp.linalg.cholesky(diagonal)  99.4 us
    another operation x16, other arithmetic, local(): inverse = jax.scipy.linalg.solve_triangular(factor, identity, lower=True)  83.9 us
    unnamed x28, local copies, waits for them, and re-layouts  51 us
    all_gather x8, blocking collectives, spread(): lax.all_gather(x_local, named_axis).sum(axis=0)  49.2 us
    dot_general x16, matrix products, product(): jnp.dot(left_rows, right_rows.T, precision=lax.Precision.HIGHEST, preferr...  29.5 us
  transfers between devices with their start and end apart: 16, of which 16 were waited for; matrix products, arithmetic and copies ran while one was open for 2% of the time, Pallas kernels for 0%

profile of v1, /device:TPU:0, one launch (start us, length us, event | category | flops | bytes accessed | tf_op | source)
XLA Modules:
  0.0 1097.1 jit_solution(17257660854374844439)
XLA Ops:
  6.5 1.8 copy.125
  8.3 7.2 all-gather
  15.7 11.7 %cholesky.134 = f32[128,128]{1,0:T(8,128)S(1)} custom-call(f32[128,128]{1,0:T(8,128)S(1)} %fusion.69), custom_call_target="Cholesky" | custom-call | tf_op jit(solution)/shard_map/jit(cholesky)/cholesky | solution.py:70
  28.7 9.8 custom-call.12
  40.7 74.4 %all-gather.49.cloned.1.call-done = f32[8192,128]{0,1:T(8,128)} async-done(((f32[1024,128]{0,1:T(8,128)}), f32[8192,128]{0,1:T(8,128)}) %all-gather.49.cloned.1.call-update) | async-done | bytes 4194320 | tf_op jit(solution)/shard_map/all_gather | solution.py:11
  115.2 5.4 copy.81
  124.0 14.4 %all-gather.33.cloned.1.call-done = f32[4,512,128]{2,1,0:T(8,128)} async-done(((f32[1,512,128]{2,1,0:T(8,128)}), f32[4,512,128]{2,1,0:T(8,128)}) %all-gather.33.cloned.1.call-update) | async-done | bytes 1048592 | tf_op jit(solution)/shard_map/all_gather | solution.py:11
  141.3 2.7 fusion.20
  144.0 6.0 all-gather.2
  150.1 11.7 %cholesky.145 = f32[128,128]{1,0:T(8,128)S(1)} custom-call(f32[128,128]{1,0:T(8,128)S(1)} %fusion.67), custom_call_target="Cholesky" | custom-call | tf_op jit(solution)/shard_map/jit(cholesky)/cholesky | solution.py:70
  163.3 9.8 custom-call.13
  175.6 73.0 %all-gather.51.cloned.1.call-done = f32[8192,128]{0,1:T(8,128)} async-done(((f32[1024,128]{0,1:T(8,128)}), f32[8192,128]{0,1:T(8,128)}) %all-gather.51.cloned.1.call-update) | async-done | bytes 4194320 | tf_op jit(solution)/shard_map/all_gather | solution.py:11
  248.7 5.4 copy.84
  257.7 14.2 %all-gather.35.cloned.1.call-done = f32[4,512,128]{2,1,0:T(8,128)} async-done(((f32[1,512,128]{2,1,0:T(8,128)}), f32[4,512,128]{2,1,0:T(8,128)}) %all-gather.35.cloned.1.call-update) | async-done | bytes 1048592 | tf_op jit(solution)/shard_map/all_gather | solution.py:11
  274.8 2.7 fusion.17
  277.5 6.0 all-gather.4
  283.6 11.7 %cholesky.156 = f32[128,128]{1,0:T(8,128)S(1)} custom-call(f32[128,128]{1,0:T(8,128)S(1)} %fusion.65), custom_call_target="Cholesky" | custom-call | tf_op jit(solution)/shard_map/jit(cholesky)/cholesky | solution.py:70
  296.7 9.8 custom-call.14
  308.7 73.3 %all-gather.53.cloned.1.call-done = f32[8192,128]{0,1:T(8,128)} async-done(((f32[1024,128]{0,1:T(8,128)}), f32[8192,128]{0,1:T(8,128)}) %all-gather.53.cloned.1.call-update) | async-done | bytes 4194320 | tf_op jit(solution)/shard_map/all_gather | solution.py:11
  382.0 5.4 copy.87
  393.3 1.9 broadcast_select_fusion.13
  396.5 10.6 all-gather.37.cloned.1.call-done
  409.4 2.6 fusion.14
  413.3 6.0 all-gather.6
  419.5 11.7 %cholesky.167 = f32[128,128]{1,0:T(8,128)S(1)} custom-call(f32[128,128]{1,0:T(8,128)S(1)} %fusion.63), custom_call_target="Cholesky" | custom-call | tf_op jit(solution)/shard_map/jit(cholesky)/cholesky | solution.py:70
  432.7 9.8 custom-call.15
  442.8 1.6 fusion.29
  446.0 73.0 %all-gather.55.cloned.1.call-done = f32[8192,128]{0,1:T(8,128)} async-done(((f32[1024,128]{0,1:T(8,128)}), f32[8192,128]{0,1:T(8,128)}) %all-gather.55.cloned.1.call-update) | async-done | bytes 4194320 | tf_op jit(solution)/shard_map/all_gather | solution.py:11
  519.1 5.4 copy.90
  528.1 14.2 %all-gather.39.cloned.1.call-done = f32[4,512,128]{2,1,0:T(8,128)} async-done(((f32[1,512,128]{2,1,0:T(8,128)}), f32[4,512,128]{2,1,0:T(8,128)}) %all-gather.39.cloned.1.call-update) | async-done | bytes 1048592 | tf_op jit(solution)/shard_map/all_gather | solution.py:11
  545.2 2.7 fusion.11
  547.9 6.0 all-gather.8
  554.0 11.7 %cholesky.178 = f32[128,128]{1,0:T(8,128)S(1)} custom-call(f32[128,128]{1,0:T(8,128)S(1)} %fusion.61), custom_call_target="Cholesky" | custom-call | tf_op jit(solution)/shard_map/jit(cholesky)/cholesky | solution.py:70
  567.1 9.8 custom-call.16
  579.1 73.3 %all-gather.57.cloned.1.call-done = f32[8192,128]{0,1:T(8,128)} async-done(((f32[1024,128]{0,1:T(8,128)}), f32[8192,128]{0,1:T(8,128)}) %all-gather.57.cloned.1.call-update) | async-done | bytes 4194320 | tf_op jit(solution)/shard_map/all_gather | solution.py:11
  652.4 5.4 copy.93
  663.7 1.9 broadcast_select_fusion.11
  666.9 10.6 all-gather.41.cloned.1.call-done
  679.8 2.6 fusion.8
  683.7 6.0 all-gather.10
  689.9 11.7 %cholesky.189 = f32[128,128]{1,0:T(8,128)S(1)} custom-call(f32[128,128]{1,0:T(8,128)S(1)} %fusion.59), custom_call_target="Cholesky" | custom-call | tf_op jit(solution)/shard_map/jit(cholesky)/cholesky | solution.py:70
  703.1 9.8 custom-call.17
  713.2 1.6 fusion.25
  716.4 73.0 %all-gather.59.cloned.1.call-done = f32[8192,128]{0,1:T(8,128)} async-done(((f32[1024,128]{0,1:T(8,128)}), f32[8192,128]{0,1:T(8,128)}) %all-gather.59.cloned.1.call-update) | async-done | bytes 4194320 | tf_op jit(solution)/shard_map/all_gather | solution.py:11
  789.5 5.4 copy.96
  798.5 14.2 %all-gather.43.cloned.1.call-done = f32[4,512,128]{2,1,0:T(8,128)} async-done(((f32[1,512,128]{2,1,0:T(8,128)}), f32[4,512,128]{2,1,0:T(8,128)}) %all-gather.43.cloned.1.call-update) | async-done | bytes 1048592 | tf_op jit(solution)/shard_map/all_gather | solution.py:11
  815.6 2.7 fusion.5
  818.4 6.0 all-gather.12
  824.4 11.7 %cholesky.200 = f32[128,128]{1,0:T(8,128)S(1)} custom-call(f32[128,128]{1,0:T(8,128)S(1)} %fusion.57), custom_call_target="Cholesky" | custom-call | tf_op jit(solution)/shard_map/jit(cholesky)/cholesky | solution.py:70
  837.6 9.8 custom-call.18
  849.7 73.3 %all-gather.61.cloned.1.call-done = f32[8192,128]{0,1:T(8,128)} async-done(((f32[1024,128]{0,1:T(8,128)}), f32[8192,128]{0,1:T(8,128)}) %all-gather.61.cloned.1.call-update) | async-done | bytes 4194320 | tf_op jit(solution)/shard_map/all_gather | solution.py:11
  923.0 5.4 copy.99
  932.0 14.2 %all-gather.45.cloned.1.call-done = f32[4,512,128]{2,1,0:T(8,128)} async-done(((f32[1,512,128]{2,1,0:T(8,128)}), f32[4,512,128]{2,1,0:T(8,128)}) %all-gather.45.cloned.1.call-update) | async-done | bytes 1048592 | tf_op jit(solution)/shard_map/all_gather | solution.py:11
  949.1 2.7 fusion.2
  951.8 6.0 all-gather.14
  958.0 11.7 %cholesky.211 = f32[128,128]{1,0:T(8,128)S(1)} custom-call(f32[128,128]{1,0:T(8,128)S(1)} %fusion.55), custom_call_target="Cholesky" | custom-call | tf_op jit(solution)/shard_map/jit(cholesky)/cholesky | solution.py:70
  971.1 9.8 custom-call.19
  983.2 73.2 %all-gather.63.cloned.1.call-done = f32[8192,128]{0,1:T(8,128)} async-done(((f32[1024,128]{0,1:T(8,128)}), f32[8192,128]{0,1:T(8,128)}) %all-gather.63.cloned.1.call-update) | async-done | bytes 4194320 | tf_op jit(solution)/shard_map/all_gather | solution.py:11
  1056.4 5.4 copy.100
  1067.4 1.9 broadcast_select_fusion.8
  1070.6 10.9 all-gather.47.cloned.1.call-done
  1082.7 3.2 convolution_subtract_fusion
  1085.9 1.9 reshape.672
  1087.9 2.2 select_select_fusion
  (277 shorter events, 90.3 us)
Async XLA Ops:
  6.5 108.6 %all-gather.49.cloned.1.call-start = ((), (), s32[]{:S(2)}) async-start(), calls=%async_computation.8 | async-start | bytes 4718592 | tf_op jit(solution)/shard_map/all_gather | solution.py:11
  40.3 98.0 %all-gather.33.cloned.1.call-start = ((), (), s32[]{:S(2)}) async-start(), calls=%async_computation | async-start | bytes 1310720 | tf_op jit(solution)/shard_map/all_gather | solution.py:11
  123.2 125.4 %all-gather.51.cloned.1.call-start = ((), (), s32[]{:S(2)}) async-start(), calls=%async_computation.9 | async-start | bytes 4718592 | tf_op jit(solution)/shard_map/all_gather | solution.py:11
  139.7 1.6 copy-start.8
  143.9 31.1 %copy-start.4 = (f32[1024,512]{1,0:T(8,128)}, f32[1024,512]{1,0:T(8,128)S(1)}, u32[]{:S(2)}) copy-start(f32[1024,512]{1,0:T(8,128)S(1)} %fusion.20) | copy-start | bytes 6291460
  175.1 96.8 %all-gather.35.cloned.1.call-start = ((), (), s32[]{:S(2)}) async-start(), calls=%async_computation.1 | async-start | bytes 1310720 | tf_op jit(solution)/shard_map/all_gather | solution.py:11
  256.7 125.3 %all-gather.53.cloned.1.call-start = ((), (), s32[]{:S(2)}) async-start(), calls=%async_computation.10 | async-start | bytes 4718592 | tf_op jit(solution)/shard_map/all_gather | solution.py:11
  273.2 1.6 copy-start.5
  308.5 98.6 %all-gather.37.cloned.1.call-start = ((), (), s32[]{:S(2)}) async-start(), calls=%async_computation.2 | async-start | bytes 1310720 | tf_op jit(solution)/shard_map/all_gather | solution.py:11
  391.9 127.2 %all-gather.55.cloned.1.call-start = ((), (), s32[]{:S(2)}) async-start(), calls=%async_computation.11 | async-start | bytes 4718592 | tf_op jit(solution)/shard_map/all_gather | solution.py:11
  412.0 1.3 copy-start.6
  445.5 96.8 %all-gather.39.cloned.1.call-start = ((), (), s32[]{:S(2)}) async-start(), calls=%async_computation.3 | async-start | bytes 1310720 | tf_op jit(solution)/shard_map/all_gather | solution.py:11
  527.1 125.3 %all-gather.57.cloned.1.call-start = ((), (), s32[]{:S(2)}) async-start(), calls=%async_computation.12 | async-start | bytes 4718592 | tf_op jit(solution)/shard_map/all_gather | solution.py:11
  543.6 1.6 copy-start.7
  578.9 98.6 %all-gather.41.cloned.1.call-start = ((), (), s32[]{:S(2)}) async-start(), calls=%async_computation.4 | async-start | bytes 1310720 | tf_op jit(solution)/shard_map/all_gather | solution.py:11
  662.3 127.2 %all-gather.59.cloned.1.call-start = ((), (), s32[]{:S(2)}) async-start(), calls=%async_computation.13 | async-start | bytes 4718592 | tf_op jit(solution)/shard_map/all_gather | solution.py:11
  682.4 1.3 copy-start
  715.9 96.8 %all-gather.43.cloned.1.call-start = ((), (), s32[]{:S(2)}) async-start(), calls=%async_computation.5 | async-start | bytes 1310720 | tf_op jit(solution)/shard_map/all_gather | solution.py:11
  797.5 125.4 %all-gather.61.cloned.1.call-start = ((), (), s32[]{:S(2)}) async-start(), calls=%async_computation.14 | async-start | bytes 4718592 | tf_op jit(solution)/shard_map/all_gather | solution.py:11
  814.0 1.6 copy-start.1
  818.3 31.1 %copy-start.2 = (f32[1024,512]{1,0:T(8,128)}, f32[1024,512]{1,0:T(8,128)S(1)}, u32[]{:S(2)}) copy-start(f32[1024,512]{1,0:T(8,128)S(1)} %fusion.5) | copy-start | bytes 6291460
  849.4 96.8 %all-gather.45.cloned.1.call-start = ((), (), s32[]{:S(2)}) async-start(), calls=%async_computation.6 | async-start | bytes 1310720 | tf_op jit(solution)/shard_map/all_gather | solution.py:11
  931.0 125.4 %all-gather.63.cloned.1.call-start = ((), (), s32[]{:S(2)}) async-start(), calls=%async_computation.15 | async-start | bytes 4718592 | tf_op jit(solution)/shard_map/all_gather | solution.py:11
  947.5 1.6 copy-start.3
  982.8 98.6 %all-gather.47.cloned.1.call-start = ((), (), s32[]{:S(2)}) async-start(), calls=%async_computation.7 | async-start | bytes 1310720 | tf_op jit(solution)/shard_map/all_gather | solution.py:11
Sparse Core Ops, SparseCore 0:
  40.4 74.6 all-gather.48
  123.3 14.9 all-gather.32
  175.2 73.4 all-gather.50
  256.9 14.9 all-gather.34
  308.6 73.3 all-gather.52
  392.0 14.9 all-gather.36
  445.6 73.3 all-gather.54
  527.3 14.9 all-gather.38
  579.0 73.4 all-gather.56
  662.4 14.9 all-gather.40
  716.0 73.4 all-gather.58
  797.7 14.9 all-gather.42
  849.5 73.4 all-gather.60
  931.2 14.9 all-gather.44
  983.0 73.4 all-gather.62
  1066.4 14.9 all-gather.46
